TPU v7x, 512 devices: a whole 4x4x16 slice. The times are simulated.
512 devices in a mesh: ctx: 32 (over x, y, core), exp: 16 (over z).
Axes of the slice: x: 4, y: 4, z: 16, core: 2. Of those that a mesh axis runs over, the one named last changes fastest.
Arguments:
- residual: bfloat16 [4096, 2048], P('ctx', 'exp'), may hold values from -60 to 60
- ssd_input: bfloat16 [4096, 2048], P('ctx', 'exp'), may hold values from -6 to 6
- state_in: bfloat16 [4096, 128], P('ctx'), may hold values from -0.015625 to 0.015625
- state_out: bfloat16 [4096, 128], P('ctx'), may hold values from -6 to 6
- log_decay: float32 [4096, 64], P('ctx', 'exp'), may hold values from -1 to 0
- skip_gain: float32 [64], P('exp'), may hold values from 0.5 to 1.5
- norm_gain: float32 [2048], P('exp'), may hold values from 0.1 to 1.9
- route_weight: float32 [4096, 2], P('ctx'), may hold values from 0.2 to 1
- expert_ids: int32 [4096, 2], P('ctx'), may hold values from 0 to 15, all different within a row; in each aligned block of 128 rows (0 to 127, 128 to 255, ...) at most 16 rows name the same one
- weight_in: bfloat16 [16, 2048, 8192], P('exp', None, 'ctx'), may hold values from -0.125 to 0.125
- weight_down: bfloat16 [16, 8192, 2048], P('exp', 'ctx'), may hold values from -0.125 to 0.125
- out_grad: bfloat16 [4096, 2048], P('ctx', 'exp'), may hold values from -6 to 6
Outputs:
- block_out: bfloat16 [4096, 2048], P('ctx', 'exp')
- grad_residual: bfloat16 [4096, 2048], P('ctx', 'exp')
- grad_input: bfloat16 [4096, 2048], P('ctx', 'exp')
- grad_weight_in: bfloat16 [16, 2048, 8192], P('exp', None, 'ctx')
- grad_weight_down: bfloat16 [16, 8192, 2048], P('exp', 'ctx')
Inputs may be any that keep to these rules, and one draw needn't show every extreme that they name: `expert_ids`: the two experts of a token differ; in each aligned block of 128 rows (the tokens of one index of ctx) every expert is named by exactly 16 rows.
All inputs are finite; a program needn't handle non-finite values.
Results may differ from a plain program's by a relative error of at most 0.015.
Values may be sent and summed in bfloat16 or wider, within the bound.
No kernel may reach another device: no remote copies, remote signals or barrier semaphores. Data moves between devices by JAX's collectives and lax.ppermute only.
A program may use at most 64 MiB of HBM per device.

v0:
```python
import jax
import jax.numpy as jnp
from jax import lax
from jax.sharding import PartitionSpec as P

D = 2048
epsilon = 1e-05
highest = lax.Precision.HIGHEST


def carried_in(value, axis, combine, identity, reverse):
    peers, index = (lax.axis_size(axis), lax.axis_index(axis))
    everything = jax.tree.map(
        lambda part, kind: lax.all_gather(part.astype(kind), axis),
        value,
        (jnp.bfloat16, jnp.bfloat16),
    )
    start = jax.tree.map(
        lambda part, zero: jnp.broadcast_to(jnp.asarray(zero, part.dtype), part.shape),
        value,
        identity,
    )

    def step(k, before):
        at = peers - 1 - k if reverse else k
        reached = at > index if reverse else at < index
        new = combine(
            before, jax.tree.map(lambda part, own: part[at].astype(own.dtype), everything, value)
        )
        return jax.tree.map(lambda a, b: jnp.where(reached, a, b), new, before)

    return lax.fori_loop(0, peers, step, start)


def carry_state(earlier, later):
    return (earlier[0] * later[0], later[0][:, None, None] * earlier[1] + later[1])


def block_mixing(log_decay, state_in_wide, state_out_wide):
    cumulative = jnp.cumsum(log_decay, axis=0)
    inner_state = jnp.dot(state_out_wide, state_in_wide.T, precision=highest)
    location_list = jnp.arange(cumulative.shape[0])
    causal = location_list[:, None] >= location_list[None, :]
    gap_log = cumulative[:, None, :] - cumulative[None, :, :]
    weights = inner_state[:, :, None] * jnp.exp(jnp.where(causal[:, :, None], gap_log, -jnp.inf))
    return (cumulative, weights)


def collect_routes(dispatch_table, returned):
    flattened = returned.reshape(-1, returned.shape[2])
    routed = lax.dot_general(
        dispatch_table, flattened, (((0,), (0,)), ((), ())), preferred_element_type=jnp.float32
    )
    return routed.reshape(-1, 2, flattened.shape[1])


def body(
    residual,
    ssd_input,
    state_in,
    state_out,
    log_decay,
    skip_gain,
    norm_gain,
    route_weight,
    expert_ids,
    weight_in,
    weight_down,
    out_grad,
):
    tokens_here = residual.shape[0]
    heads_here = log_decay.shape[1]
    feature_width = residual.shape[1]
    head_width = feature_width // heads_here
    exp_count = lax.axis_size("exp")
    capacity = 2 * tokens_here // exp_count
    state_in_wide = state_in.astype(jnp.float32)
    state_out_wide = state_out.astype(jnp.float32)
    cumulative, weights = block_mixing(log_decay, state_in_wide, state_out_wide)
    head_input = ssd_input.astype(jnp.float32).reshape(tokens_here, heads_here, head_width)
    ending = cumulative[-1]
    tail_decay = jnp.exp(ending[None, :] - cumulative)
    block_state = jnp.einsum(
        "sh,sn,shp->hnp", tail_decay, state_in_wide, head_input, precision=highest
    )
    block_decay = jnp.exp(ending)
    identity = (jnp.ones_like(block_decay), jnp.zeros_like(block_state))
    incoming = carried_in((block_decay, block_state), "ctx", carry_state, identity, False)[1]
    ssd_out = jnp.einsum("tsh,shp->thp", weights, head_input, precision=highest)
    ssd_out = ssd_out + jnp.exp(cumulative)[:, :, None] * jnp.einsum(
        "tn,hnp->thp", state_out_wide, incoming, precision=highest
    )
    ssd_out = ssd_out + skip_gain[None, :, None] * head_input
    mixed = (residual.astype(jnp.float32) + ssd_out.reshape(tokens_here, feature_width)).astype(
        jnp.bfloat16
    )
    mixed_wide = mixed.astype(jnp.float32)
    square_sum = lax.psum(jnp.sum(mixed_wide * mixed_wide, axis=1), "exp")
    inv_rms = lax.rsqrt(square_sum / D + epsilon)[:, None]
    normed = (mixed_wide * inv_rms * norm_gain[None, :]).astype(jnp.bfloat16)
    route_ids = expert_ids.reshape(-1)
    onehot = (route_ids[:, None] == jnp.arange(exp_count)[None, :]).astype(jnp.int32)
    before = jnp.cumsum(onehot, axis=0) - onehot
    slot_index = jnp.sum(before * onehot, axis=1)
    target = route_ids * capacity + slot_index
    dispatch_table = (jnp.arange(exp_count * capacity)[:, None] == target[None, :]).astype(
        jnp.bfloat16
    )
    route_rows = jnp.repeat(normed, 2, axis=0)
    out_grad_wide = out_grad.astype(jnp.float32)
    route_cot = (route_weight.reshape(-1)[:, None] * jnp.repeat(out_grad_wide, 2, axis=0)).astype(
        jnp.bfloat16
    )
    spread_rows = (
        jnp.dot(dispatch_table, route_rows, preferred_element_type=jnp.float32)
        .astype(jnp.bfloat16)
        .reshape(exp_count, capacity, feature_width)
    )
    spread_cot = (
        jnp.dot(dispatch_table, route_cot, preferred_element_type=jnp.float32)
        .astype(jnp.bfloat16)
        .reshape(exp_count, capacity, feature_width)
    )
    arrived_rows, arrived_cot = (
        lax.all_to_all(spread_rows, "exp", split_axis=0, concat_axis=2, tiled=True),
        lax.all_to_all(spread_cot, "exp", split_axis=0, concat_axis=2, tiled=True),
    )
    expert_rows, cot_rows = (
        lax.all_gather(arrived_rows[0], "ctx", axis=0, tiled=True),
        lax.all_gather(arrived_cot[0], "ctx", axis=0, tiled=True),
    )
    matrix_in = weight_in[0]
    matrix_down = weight_down[0]
    hidden = jnp.dot(expert_rows, matrix_in, preferred_element_type=jnp.float32)
    activated = jax.nn.silu(hidden).astype(jnp.bfloat16)
    row_piece = activated
    out_rows = lax.psum_scatter(
        jnp.dot(row_piece, matrix_down, preferred_element_type=jnp.float32).astype(jnp.bfloat16),
        "ctx",
        scatter_dimension=0,
        tiled=True,
    )
    returned = lax.all_to_all(out_rows[None], "exp", split_axis=2, concat_axis=0, tiled=True)
    routed = collect_routes(dispatch_table, returned)
    expert_mix = jnp.sum(routed * route_weight[:, :, None], axis=1)
    block_out = (mixed_wide + expert_mix).astype(jnp.bfloat16)
    d_act = lax.dot_general(
        cot_rows, matrix_down, (((1,), (1,)), ((), ())), preferred_element_type=jnp.float32
    )
    sigmoid_h = jax.nn.sigmoid(hidden)
    d_hidden = (d_act * sigmoid_h * (1.0 + hidden * (1.0 - sigmoid_h))).astype(jnp.bfloat16)
    grad_down = lax.dot_general(
        activated, cot_rows, (((0,), (0,)), ((), ())), preferred_element_type=jnp.float32
    )
    grad_in = lax.dot_general(
        expert_rows, d_hidden, (((0,), (0,)), ((), ())), preferred_element_type=jnp.float32
    )
    row_piece = d_hidden
    d_rows = lax.psum_scatter(
        lax.dot_general(
            row_piece, matrix_in, (((1,), (1,)), ((), ())), preferred_element_type=jnp.float32
        ).astype(jnp.bfloat16),
        "ctx",
        scatter_dimension=0,
        tiled=True,
    )
    returned_grads = lax.all_to_all(d_rows[None], "exp", split_axis=2, concat_axis=0, tiled=True)
    d_normed = jnp.sum(collect_routes(dispatch_table, returned_grads), axis=1)
    scaled = norm_gain[None, :] * d_normed
    dot_terms = lax.psum(jnp.sum(scaled * mixed_wide, axis=1), "exp")[:, None]
    d_mixed = (
        out_grad_wide + inv_rms * scaled - mixed_wide * inv_rms * inv_rms * inv_rms * dot_terms / D
    )
    head_grad = d_mixed.reshape(tokens_here, heads_here, head_width)
    grad_heads = jnp.einsum("tsh,thp->shp", weights, head_grad, precision=highest)
    lead_decay = jnp.exp(cumulative)
    block_cot = jnp.einsum(
        "th,tn,thp->hnp", lead_decay, state_out_wide, head_grad, precision=highest
    )
    later_state = carried_in((block_decay, block_cot), "ctx", carry_state, identity, True)[1]
    grad_heads = grad_heads + tail_decay[:, :, None] * jnp.einsum(
        "sn,hnp->shp", state_in_wide, later_state, precision=highest
    )
    grad_heads = grad_heads + skip_gain[None, :, None] * head_grad
    grad_input = grad_heads.reshape(tokens_here, feature_width).astype(jnp.bfloat16)
    return (
        block_out,
        d_mixed.astype(jnp.bfloat16),
        grad_input,
        grad_in.astype(jnp.bfloat16)[None],
        grad_down.astype(jnp.bfloat16)[None],
    )


def solution(mesh):
    placed = (
        P("ctx", "exp"),
        P("ctx", "exp"),
        P("ctx", None),
        P("ctx", None),
        P("ctx", "exp"),
        P("exp"),
        P("exp"),
        P("ctx", None),
        P("ctx", None),
        P("exp", None, "ctx"),
        P("exp", "ctx", None),
        P("ctx", "exp"),
    )
    return jax.shard_map(
        body,
        mesh=mesh,
        in_specs=placed,
        out_specs=(
            P("ctx", "exp"),
            P("ctx", "exp"),
            P("ctx", "exp"),
            P("exp", None, "ctx"),
            P("exp", "ctx", None),
        ),
        check_vma=False,
    )
```

profile of v0, /device:TPU:1, one launch (start us, length us, event | category | flops | bytes accessed | tf_op | source)
XLA Modules:
  0.0 650.2 jit_solution(7748751069555235195)
XLA Ops:
  12.9 24.1 %all-gather.2 = bf16[32,1,4]{2,1,0:T(2,128)(2,1)S(1)} all-gather(bf16[1,1,4]{2,1,0:T(2,128)(2,1)S(1)} %get-tuple-element.356), channel_id=1, replica_groups=mesh['ctx'=32,'exp'=16] {'ctx'}, dimensions={0}, use_global_device_ids=true | all-gather | bytes 264 | tf_op jit(solution)/shard_map/all_gather | solution.py:14
  38.3 37.0 %all-gather.12.cloned.1.call-done = bf16[128,128,32]{1,2,0:T(8,128)(2,1)} async-done(((bf16[4,128,32]{1,2,0:T(8,128)(2,1)}), bf16[128,128,32]{1,2,0:T(8,128)(2,1)}) %all-gather.12.cloned.1.call-update) | async-done | bytes 1048592 | tf_op jit(solution)/shard_map/all_gather | solution.py:14
  75.3 33.7 %while.30 = (s32[]{:T(128)}, f32[4,128,32]{2,1,0:T(8,128)S(1)}, s32[]{:T(128)}, bf16[32,4]{1,0:T(8,128)(2,1)S(1)}, bf16[32,4,128,32]{2,3,1,0:T(8,128)(2,1)}, /*index=5*/s32[]{:T(128)}, s32[]{:T(128)}) while((s32[]{:T(128)}, f32[4,128,32]{2,1,0:T(8,128)S(1)}, s32[]{:T(128)}, bf16[32,4]{1,0:T(8,128)(2,1)S(1)}, ...), condition=%wide.region_2.3_spmd.clone, body=%wide.region_1.2_spmd.clone.sunk | while | flops 81928 | bytes 295065 | solution.py:32
  110.1 24.8 %psum.14 = f32[128]{0:T(128)S(1)} all-reduce(f32[128]{0:T(128)S(1)} %get-tuple-element.351), channel_id=1, replica_groups=mesh['ctx'=32,'exp'=16] {'exp'}, use_global_device_ids=true, to_apply=%region_7.8 | all-reduce | flops 128 | bytes 1024 | tf_op jit(solution)/shard_map/psum | solution.py:98
  135.2 19.0 %all_to_all.60 = bf16[16,16,128]{2,1,0:T(8,128)(2,1)S(1)} all-to-all(bf16[16,16,128]{2,1,0:T(8,128)(2,1)S(1)} %bitcast.189), channel_id=1, replica_groups=mesh['ctx'=32,'exp'=16] {'exp'}, dimensions={0} | all-to-all | bytes 131072 | tf_op jit(solution)/shard_map/all_to_all | solution.py:125
  155.6 14.2 %all_to_all.61 = bf16[16,16,128]{2,1,0:T(8,128)(2,1)S(1)} all-to-all(bf16[16,16,128]{2,1,0:T(8,128)(2,1)S(1)} %bitcast.168), channel_id=1, replica_groups=mesh['ctx'=32,'exp'=16] {'exp'}, dimensions={0} | all-to-all | bytes 131072 | tf_op jit(solution)/shard_map/all_to_all | solution.py:126
  170.6 42.3 %all-gather.8.cloned.1.call-done = bf16[512,2048]{1,0:T(8,128)(2,1)} async-done(((bf16[16,2048]{1,0:T(8,128)(2,1)}), bf16[512,2048]{1,0:T(8,128)(2,1)}) %all-gather.8.cloned.1.call-update) | async-done | bytes 2097168 | tf_op jit(solution)/shard_map/all_gather | solution.py:129
  212.9 2.3 fusion.19
  215.2 2.1 convolution_convert_fusion.1
  217.6 57.4 %all-gather.10.cloned.1.call-done = bf16[512,2048]{1,0:T(8,128)(2,1)} async-done(((bf16[16,2048]{1,0:T(8,128)(2,1)}), bf16[512,2048]{1,0:T(8,128)(2,1)}) %all-gather.10.cloned.1.call-update) | async-done | bytes 2097168 | tf_op jit(solution)/shard_map/all_gather | solution.py:130
  274.9 2.4 fusion.5
  277.3 2.1 convolution_convert_fusion
  279.4 99.2 %reduce-scatter.3.cloned.1.call-done = bf16[16,2048]{1,0:T(8,128)(2,1)} async-done(((bf16[512,2048]{1,0:T(8,128)(2,1)}), bf16[16,2048]{1,0:T(8,128)(2,1)}) %reduce-scatter.3.cloned.1.call-update) | async-done | bytes 65552 | tf_op jit(solution)/shard_map/reduce_scatter | solution.py:137
  378.6 2.0 copy.104
  381.1 11.5 %reduce.3 = bf16[2048,16]{1,0:T(8,128)(2,1)S(1)} reduce(bf16[2048,1,16]{2,1,0:T(2,128)(2,1)S(1)} %bitcast.163, bf16[]{:T(256)} %broadcast.81), dimensions={1}, to_apply=%bitcast.131.reduce_sub_computation | reduce | bytes 131074
  393.8 12.0 %all-to-all-start.1 = ((bf16[16,2,1024]{2,1,0:T(2,128)(2,1)}), bf16[16,2,1024]{2,1,0:T(2,128)(2,1)S(1)}, u32[]{:S(2)}, u32[]{:S(2)}) async-start(bf16[16,2,1024]{2,1,0:T(2,128)(2,1)} %reshape.206), calls=%async_computation.2 | async-start | bytes 131072 | tf_op jit(solution)/shard_map/all_to_all | solution.py:143
  405.8 78.6 %reduce-scatter.5.cloned.1.call-done = bf16[16,2048]{1,0:T(8,128)(2,1)} async-done(((bf16[512,2048]{1,0:T(8,128)(2,1)}), bf16[16,2048]{1,0:T(8,128)(2,1)}) %reduce-scatter.5.cloned.1.call-update) | async-done | bytes 65552 | tf_op jit(solution)/shard_map/reduce_scatter | solution.py:159
  486.4 11.5 %reduce.2 = bf16[2048,16]{1,0:T(8,128)(2,1)S(1)} reduce(bf16[2048,1,16]{2,1,0:T(2,128)(2,1)S(1)} %bitcast.164, bf16[]{:T(256)} %broadcast.81), dimensions={1}, to_apply=%bitcast.133.reduce_sub_computation | reduce | bytes 131074
  499.1 12.0 %all-to-all-start.3 = ((bf16[16,2,1024]{2,1,0:T(2,128)(2,1)}), bf16[16,2,1024]{2,1,0:T(2,128)(2,1)S(1)}, u32[]{:S(2)}, u32[]{:S(2)}) async-start(bf16[16,2,1024]{2,1,0:T(2,128)(2,1)} %reshape.208), calls=%async_computation.5 | async-start | bytes 131072 | tf_op jit(solution)/shard_map/all_to_all | solution.py:167
  512.9 9.8 %all-to-all-done.3 = bf16[16,2,1024]{2,1,0:T(2,128)(2,1)S(1)} async-done(((bf16[16,2,1024]{2,1,0:T(2,128)(2,1)}), bf16[16,2,1024]{2,1,0:T(2,128)(2,1)S(1)}, u32[]{:S(2)}, u32[]{:S(2)}) %all-to-all-start.3) | async-done | bytes 65568 | tf_op jit(solution)/shard_map/all_to_all | solution.py:167
  524.7 21.7 %psum.15 = f32[128]{0:T(128)S(1)} all-reduce(f32[128]{0:T(128)S(1)} %fusion.44), channel_id=1, replica_groups=mesh['ctx'=32,'exp'=16] {'exp'}, use_global_device_ids=true, to_apply=%region_13.14 | all-reduce | flops 128 | bytes 1024 | tf_op jit(solution)/shard_map/psum | solution.py:170
  548.1 3.5 fusion.2
  553.4 54.5 %all-gather.14.cloned.1.call-done = bf16[128,128,32]{1,2,0:T(8,128)(2,1)} async-done(((bf16[4,128,32]{1,2,0:T(8,128)(2,1)}), bf16[128,128,32]{1,2,0:T(8,128)(2,1)}) %all-gather.14.cloned.1.call-update) | async-done | bytes 1048592 | tf_op jit(solution)/shard_map/all_gather | solution.py:14
  607.9 33.9 %while.31 = (s32[]{:T(128)}, f32[4,128,32]{2,1,0:T(8,128)S(1)}, s32[]{:T(128)}, bf16[32,4]{1,0:T(8,128)(2,1)S(1)}, bf16[32,4,128,32]{2,3,1,0:T(8,128)(2,1)}, /*index=5*/s32[]{:T(128)}, s32[]{:T(128)}, s32[]{:T(128)}, s32[]{:T(128)}) while((s32[]{:T(128)}, f32[4,128,32]{2,1,0:T(8,128)S(1)}, s32[]{:T(128)}, ...), condition=%wide.region_15.16_spmd.clone, body=%wide.region_14.15_spmd.clone.sunk | while | flops 81932 | bytes 295127 | solution.py:32
  (360 shorter events, 89.0 us)
Async XLA Ops:
  7.2 208.0 %copy-start = (bf16[1,256,2048]{2,1,0:T(8,128)(2,1)S(1)}, bf16[1,256,2048]{2,1,0:T(8,128)(2,1)}, u32[]{:S(2)}) copy-start(bf16[1,256,2048]{2,1,0:T(8,128)(2,1)} %param.26) | copy-start | bytes 3145732
  7.2 68.1 %all-gather.12.cloned.1.call-start = ((), (), s32[]{:S(2)}) async-start(), calls=%async_computation.10 | async-start | bytes 1081344 | tf_op jit(solution)/shard_map/all_gather | solution.py:14
  10.8 202.0 %all-gather.8.cloned.1.call-start = ((), (), s32[]{:S(2)}) async-start(), calls=%async_computation.6 | async-start | bytes 2162688 | tf_op jit(solution)/shard_map/all_gather | solution.py:129
  75.3 33.8 %copy-start.3 = (bf16[128,128]{1,0:T(8,128)(2,1)S(1)}, bf16[128,128]{1,0:T(8,128)(2,1)}, u32[]{:S(2)}) copy-start(bf16[128,128]{1,0:T(8,128)(2,1)} %param.19) | copy-start | bytes 98308
  75.3 34.2 %copy-start.9 = (f32[4]{0:T(128)S(1)}, f32[4]{0:T(128)}, u32[]{:S(2)}) copy-start(f32[4]{0:T(128)} %param.21) | copy-start | bytes 52
  75.3 34.7 %copy-start.5 = (bf16[128,128]{1,0:T(8,128)(2,1)S(1)}, bf16[128,128]{1,0:T(8,128)(2,1)}, u32[]{:S(2)}) copy-start(bf16[128,128]{1,0:T(8,128)(2,1)} %param.16) | copy-start | bytes 98308
  75.3 59.6 %copy-start.6 = (f32[128]{0:T(128)S(1)}, f32[128]{0:T(128)}, u32[]{:S(2)}) copy-start(f32[128]{0:T(128)} %param.22) | copy-start | bytes 1540
  75.3 79.7 %copy-start.7 = (f32[128,2]{0,1:T(2,128)S(1)}, f32[128,2]{0,1:T(2,128)}, u32[]{:S(2)}) copy-start(f32[128,2]{0,1:T(2,128)} %param.23) | copy-start | bytes 3076
  75.3 80.0 %copy-start.4 = (bf16[128,128]{1,0:T(8,128)(2,1)S(1)}, bf16[128,128]{1,0:T(8,128)(2,1)}, u32[]{:S(2)}) copy-start(bf16[128,128]{1,0:T(8,128)(2,1)} %param.27) | copy-start | bytes 98308
  109.0 103.8 %copy-start.1 = (bf16[1,2048,256]{2,1,0:T(8,128)(2,1)S(1)}, bf16[1,2048,256]{2,1,0:T(8,128)(2,1)}, u32[]{:S(2)}) copy-start(bf16[1,2048,256]{2,1,0:T(8,128)(2,1)} %param.25) | copy-start | bytes 3145732
  154.9 120.0 %all-gather.10.cloned.1.call-start = ((), (), s32[]{:S(2)}) async-start(), calls=%async_computation.8 | async-start | bytes 2162688 | tf_op jit(solution)/shard_map/all_gather | solution.py:130
  170.5 208.1 %reduce-scatter.3.cloned.1.call-start = ((), (), s32[]{:S(2)}) async-start(), calls=%async_computation.7 | async-start | bytes 2162688 | tf_op jit(solution)/shard_map/reduce_scatter | solution.py:137
  215.2 59.7 %copy-start.10 = (f32[512,256]{1,0:T(8,128)}, f32[512,256]{1,0:T(8,128)S(1)}, u32[]{:S(2)}) copy-start(f32[512,256]{1,0:T(8,128)S(1)} %fusion.19) | copy-start | bytes 1572868
  217.3 267.1 %reduce-scatter.5.cloned.1.call-start = ((), (), s32[]{:S(2)}) async-start(), calls=%async_computation.9 | async-start | bytes 2162688 | tf_op jit(solution)/shard_map/reduce_scatter | solution.py:159
  393.8 105.3 %all-to-all-start.1 = ((bf16[16,2,1024]{2,1,0:T(2,128)(2,1)}), bf16[16,2,1024]{2,1,0:T(2,128)(2,1)S(1)}, u32[]{:S(2)}, u32[]{:S(2)}) async-start(bf16[16,2,1024]{2,1,0:T(2,128)(2,1)} %reshape.206), calls=%async_computation.2 | async-start | bytes 131072 | tf_op jit(solution)/shard_map/all_to_all | solution.py:143
  499.1 23.6 %all-to-all-start.3 = ((bf16[16,2,1024]{2,1,0:T(2,128)(2,1)}), bf16[16,2,1024]{2,1,0:T(2,128)(2,1)S(1)}, u32[]{:S(2)}, u32[]{:S(2)}) async-start(bf16[16,2,1024]{2,1,0:T(2,128)(2,1)} %reshape.208), calls=%async_computation.5 | async-start | bytes 131072 | tf_op jit(solution)/shard_map/all_to_all | solution.py:167
  511.2 96.7 %all-gather.14.cloned.1.call-start = ((), (), s32[]{:S(2)}) async-start(), calls=%async_computation.11 | async-start | bytes 1081344 | tf_op jit(solution)/shard_map/all_gather | solution.py:14
  548.1 3.5 copy-start.8
  548.1 3.5 copy-start.11
  607.9 33.9 %copy-start.2 = (bf16[128,128]{1,0:T(8,128)(2,1)S(1)}, bf16[128,128]{1,0:T(8,128)(2,1)}, u32[]{:S(2)}) copy-start(bf16[128,128]{1,0:T(8,128)(2,1)} %param.18) | copy-start | bytes 98308
Sparse Core Ops, SparseCore 0:
  11.7 63.5 all-gather.11
  155.1 57.7 all-gather.7
  216.6 58.3 all-gather.9
  279.2 99.3 reduce-scatter.2
  382.9 101.5 reduce-scatter.4
  548.2 59.5 all-gather.13
where the time goes:
time: 655 us; the launch traced here: 650 us
  waiting for transfers between devices  379 us (58%)
  blocking collectives  104 us (16%)
  local copies, waits for them, and re-layouts  73.3 us (11%)
  other arithmetic  32.8 us (5%)
  starting transfers between devices  24.5 us (4%)
  matrix products  19.7 us (3%)
  between operations  14.5 us (2%)
    reduce_scatter x1, waiting for transfers between devices, body(): lax.psum_scatter(jnp.dot(row_piece, matrix_down, preferred_element_type=j...  99.2 us
    all_gather x2, waiting for transfers between devices, carried_in(): lax.all_gather(part.astype(kind), axis)  91.5 us
    reduce_scatter x1, waiting for transfers between devices, body(): lax.psum_scatter(lax.dot_general(row_piece, matrix_in, (((1,), (1,)), (()...  78.6 us
    dynamic_slice x128, local copies, waits for them, and re-layouts, step(): part[at].astype(own.dtype)  57.5 us
    all_gather x1, waiting for transfers between devices, body(): lax.all_gather(arrived_cot[0], 'ctx', axis=0, tiled=True)  57.4 us
    all_gather x1, waiting for transfers between devices, body(): lax.all_gather(arrived_rows[0], 'ctx', axis=0, tiled=True)  42.3 us
    psum x1, blocking collectives, body(): square_sum = lax.psum(jnp.sum(mixed_wide * mixed_wide, axis=1), 'exp')  24.8 us
    all_gather x1, blocking collectives, carried_in(): lax.all_gather(part.astype(kind), axis)  24.1 us
  transfers between devices with their start and end apart: 8, of which 7 were waited for; matrix products, arithmetic and copies ran while one was open for 8% of the time, Pallas kernels for 0%

commit v1 on v0

--- a/solution.py
+++ b/solution.py
@@ -126,7 +126,9 @@
         lax.all_to_all(spread_cot, "exp", split_axis=0, concat_axis=2, tiled=True),
     )
     expert_rows, cot_rows = (
-        lax.all_gather(arrived_rows[0], "ctx", axis=0, tiled=True),
+        jnp.concatenate(
+            lax.all_to_all(jnp.stack([arrived_rows[0]] * lax.axis_size("ctx")), "ctx", 0, 0), axis=0
+        ),
         lax.all_gather(arrived_cot[0], "ctx", axis=0, tiled=True),
     )
     matrix_in = weight_in[0]

time: 655 us -> 566 us (0.86)
  waiting for transfers between devices: 379 us -> 246 us
  blocking collectives: 104 us -> 130 us
  starting transfers between devices: 24.5 us -> 40.2 us
    all_gather x1, waiting for transfers between devices: 57.4 us -> 0.02 us  [body(): lax.all_gather(arrived_cot[0], 'ctx', axis=0, tiled=True)]
    all_gather x1 -> x0, waiting for transfers between devices: 42.3 us -> none  [body(): lax.all_gather(arrived_rows[0], 'ctx', axis=0, tiled=True)]
    all_to_all x1, blocking collectives: 14.2 us -> 41.4 us  [body(): lax.all_to_all(jnp.stack([arrived_rows[0]] * lax.axis_size('ctx')), 'ctx'...]
    all_gather x2, waiting for transfers between devices: 91.5 us -> 73.7 us  [carried_in(): lax.all_gather(part.astype(kind), axis)]
    all_to_all x0 -> x1, starting transfers between devices: none -> 15.7 us  [body(): lax.all_to_all(spread_cot, 'exp', split_axis=0, concat_axis=2, tiled=True)]
    reduce_scatter x1, waiting for transfers between devices: 99.2 us -> 84.1 us  [body(): lax.psum_scatter(jnp.dot(row_piece, matrix_down, preferred_element_type=j...]
  transfers between devices with their start and end apart: 8 -> 8, of which waited for: 7 -> 5; matrix products, arithmetic and copies ran while one was open for 8% -> 15% of each run, Pallas kernels for 0% -> 0%
where the time goes in v1:
time: 566 us; the launch traced here: 561 us
  waiting for transfers between devices  246 us (43%)
  blocking collectives  130 us (23%)
  local copies, waits for them, and re-layouts  75.6 us (13%)
  starting transfers between devices  40.2 us (7%)
  other arithmetic  32.8 us (6%)
  matrix products  18.8 us (3%)
  between operations  14.3 us (3%)
    reduce_scatter x1, waiting for transfers between devices, body(): lax.psum_scatter(jnp.dot(row_piece, matrix_down, preferred_element_type=j...  84.1 us
    reduce_scatter x1, waiting for transfers between devices, body(): lax.psum_scatter(lax.dot_general(row_piece, matrix_in, (((1,), (1,)), (()...  78.5 us
    all_gather x2, waiting for transfers between devices, carried_in(): lax.all_gather(part.astype(kind), axis)  73.7 us
    dynamic_slice x128, local copies, waits for them, and re-layouts, step(): part[at].astype(own.dtype)  57.4 us
    all_to_all x1, blocking collectives, body(): lax.all_to_all(jnp.stack([arrived_rows[0]] * lax.axis_size('ctx')), 'ctx'...  41.4 us
    psum x1, blocking collectives, body(): square_sum = lax.psum(jnp.sum(mixed_wide * mixed_wide, axis=1), 'exp')  25.6 us
    unnamed x4, other arithmetic  23.1 us
    all_gather x1, blocking collectives, carried_in(): lax.all_gather(part.astype(kind), axis)  22.6 us
  transfers between devices with their start and end apart: 8, of which 5 were waited for; matrix products, arithmetic and copies ran while one was open for 15% of the time, Pallas kernels for 0%

profile of v1, /device:TPU:1, one launch (start us, length us, event | category | flops | bytes accessed | tf_op | source)
XLA Modules:
  0.0 560.9 jit_solution(13237454421964409151)
XLA Ops:
  15.5 15.7 %all-to-all-start.3 = ((bf16[16,16,128]{2,1,0:T(8,128)(2,1)}), bf16[16,16,128]{2,1,0:T(8,128)(2,1)S(1)}, u32[]{:S(2)}, u32[]{:S(2)}) async-start(bf16[16,16,128]{2,1,0:T(8,128)(2,1)} %bitcast.24), calls=%async_computation.4 | async-start | bytes 131072 | tf_op jit(solution)/shard_map/all_to_all | solution.py:126
  31.3 22.6 %all-gather.2 = bf16[32,1,4]{2,1,0:T(2,128)(2,1)S(1)} all-gather(bf16[1,1,4]{2,1,0:T(2,128)(2,1)S(1)} %get-tuple-element.356), channel_id=1, replica_groups=mesh['ctx'=32,'exp'=16] {'ctx'}, dimensions={0}, use_global_device_ids=true | all-gather | bytes 264 | tf_op jit(solution)/shard_map/all_gather | solution.py:14
  55.9 19.3 %all-gather.9.cloned.1.call-done = bf16[128,128,32]{1,2,0:T(8,128)(2,1)} async-done(((bf16[4,128,32]{1,2,0:T(8,128)(2,1)}), bf16[128,128,32]{1,2,0:T(8,128)(2,1)}) %all-gather.9.cloned.1.call-update) | async-done | bytes 1048592 | tf_op jit(solution)/shard_map/all_gather | solution.py:14
  75.3 33.7 %while.30 = (s32[]{:T(128)}, f32[4,128,32]{2,1,0:T(8,128)S(1)}, s32[]{:T(128)}, bf16[32,4]{1,0:T(8,128)(2,1)S(1)}, bf16[32,4,128,32]{2,3,1,0:T(8,128)(2,1)}, /*index=5*/s32[]{:T(128)}, s32[]{:T(128)}) while((s32[]{:T(128)}, f32[4,128,32]{2,1,0:T(8,128)S(1)}, s32[]{:T(128)}, bf16[32,4]{1,0:T(8,128)(2,1)S(1)}, ...), condition=%wide.region_2.3_spmd.clone, body=%wide.region_1.2_spmd.clone.sunk | while | flops 81928 | bytes 295065 | solution.py:32
  110.0 25.6 %psum.14 = f32[128]{0:T(128)S(1)} all-reduce(f32[128]{0:T(128)S(1)} %get-tuple-element.351), channel_id=1, replica_groups=mesh['ctx'=32,'exp'=16] {'exp'}, use_global_device_ids=true, to_apply=%region_7.8 | all-reduce | flops 128 | bytes 1024 | tf_op jit(solution)/shard_map/psum | solution.py:98
  136.0 19.0 %all_to_all.68 = bf16[16,16,128]{2,1,0:T(8,128)(2,1)S(1)} all-to-all(bf16[16,16,128]{2,1,0:T(8,128)(2,1)S(1)} %bitcast.191), channel_id=1, replica_groups=mesh['ctx'=32,'exp'=16] {'exp'}, dimensions={0} | all-to-all | bytes 131072 | tf_op jit(solution)/shard_map/all_to_all | solution.py:125
  155.3 41.4 %all_to_all.69 = bf16[32,16,2048]{2,1,0:T(8,128)(2,1)S(1)} all-to-all(bf16[32,16,2048]{2,1,0:T(8,128)(2,1)S(1)} %stack.3), channel_id=1, replica_groups=mesh['ctx'=32,'exp'=16] {'ctx'}, dimensions={0} | all-to-all | bytes 4194304 | tf_op jit(solution)/shard_map/all_to_all | solution.py:130
  198.7 2.1 convolution_convert_fusion.1
  201.1 2.3 fusion.5
  203.4 2.1 convolution_convert_fusion
  205.5 84.1 %reduce-scatter.3.cloned.1.call-done = bf16[16,2048]{1,0:T(8,128)(2,1)} async-done(((bf16[512,2048]{1,0:T(8,128)(2,1)}), bf16[16,2048]{1,0:T(8,128)(2,1)}) %reduce-scatter.3.cloned.1.call-update) | async-done | bytes 65552 | tf_op jit(solution)/shard_map/reduce_scatter | solution.py:139
  289.6 2.0 copy.104
  292.1 11.5 %reduce.3 = bf16[2048,16]{1,0:T(8,128)(2,1)S(1)} reduce(bf16[2048,1,16]{2,1,0:T(2,128)(2,1)S(1)} %bitcast.164, bf16[]{:T(256)} %broadcast.82), dimensions={1}, to_apply=%bitcast.132.reduce_sub_computation | reduce | bytes 131074
  304.8 12.0 %all-to-all-start.2 = ((bf16[16,2,1024]{2,1,0:T(2,128)(2,1)}), bf16[16,2,1024]{2,1,0:T(2,128)(2,1)S(1)}, u32[]{:S(2)}, u32[]{:S(2)}) async-start(bf16[16,2,1024]{2,1,0:T(2,128)(2,1)} %reshape.211), calls=%async_computation.3 | async-start | bytes 131072 | tf_op jit(solution)/shard_map/all_to_all | solution.py:145
  316.9 78.5 %reduce-scatter.5.cloned.1.call-done = bf16[16,2048]{1,0:T(8,128)(2,1)} async-done(((bf16[512,2048]{1,0:T(8,128)(2,1)}), bf16[16,2048]{1,0:T(8,128)(2,1)}) %reduce-scatter.5.cloned.1.call-update) | async-done | bytes 65552 | tf_op jit(solution)/shard_map/reduce_scatter | solution.py:161
  395.4 2.0 copy.110
  397.4 11.5 %reduce.2 = bf16[2048,16]{1,0:T(8,128)(2,1)S(1)} reduce(bf16[2048,1,16]{2,1,0:T(2,128)(2,1)S(1)} %bitcast.165, bf16[]{:T(256)} %broadcast.82), dimensions={1}, to_apply=%bitcast.134.reduce_sub_computation | reduce | bytes 131074
  410.1 12.0 %all-to-all-start.4 = ((bf16[16,2,1024]{2,1,0:T(2,128)(2,1)}), bf16[16,2,1024]{2,1,0:T(2,128)(2,1)S(1)}, u32[]{:S(2)}, u32[]{:S(2)}) async-start(bf16[16,2,1024]{2,1,0:T(2,128)(2,1)} %reshape.213), calls=%async_computation.6 | async-start | bytes 131072 | tf_op jit(solution)/shard_map/all_to_all | solution.py:169
  423.9 9.8 %all-to-all-done.4 = bf16[16,2,1024]{2,1,0:T(2,128)(2,1)S(1)} async-done(((bf16[16,2,1024]{2,1,0:T(2,128)(2,1)}), bf16[16,2,1024]{2,1,0:T(2,128)(2,1)S(1)}, u32[]{:S(2)}, u32[]{:S(2)}) %all-to-all-start.4) | async-done | bytes 65568 | tf_op jit(solution)/shard_map/all_to_all | solution.py:169
  435.7 21.8 %psum.15 = f32[128]{0:T(128)S(1)} all-reduce(f32[128]{0:T(128)S(1)} %fusion.44), channel_id=1, replica_groups=mesh['ctx'=32,'exp'=16] {'exp'}, use_global_device_ids=true, to_apply=%region_13.14 | all-reduce | flops 128 | bytes 1024 | tf_op jit(solution)/shard_map/psum | solution.py:172
  459.2 3.5 fusion.2
  462.6 1.7 fusion.3
  464.4 54.4 %all-gather.11.cloned.1.call-done = bf16[128,128,32]{1,2,0:T(8,128)(2,1)} async-done(((bf16[4,128,32]{1,2,0:T(8,128)(2,1)}), bf16[128,128,32]{1,2,0:T(8,128)(2,1)}) %all-gather.11.cloned.1.call-update) | async-done | bytes 1048592 | tf_op jit(solution)/shard_map/all_gather | solution.py:14
  518.8 34.0 %while.31 = (s32[]{:T(128)}, f32[4,128,32]{2,1,0:T(8,128)S(1)}, s32[]{:T(128)}, bf16[32,4]{1,0:T(8,128)(2,1)S(1)}, bf16[32,4,128,32]{2,3,1,0:T(8,128)(2,1)}, /*index=5*/s32[]{:T(128)}, s32[]{:T(128)}, s32[]{:T(128)}, s32[]{:T(128)}) while((s32[]{:T(128)}, f32[4,128,32]{2,1,0:T(8,128)S(1)}, s32[]{:T(128)}, ...), condition=%wide.region_15.16_spmd.clone, body=%wide.region_14.15_spmd.clone.sunk | while | flops 81932 | bytes 295127 | solution.py:32
  (362 shorter events, 88.9 us)
Async XLA Ops:
  7.2 191.5 %copy-start = (bf16[1,256,2048]{2,1,0:T(8,128)(2,1)S(1)}, bf16[1,256,2048]{2,1,0:T(8,128)(2,1)}, u32[]{:S(2)}) copy-start(bf16[1,256,2048]{2,1,0:T(8,128)(2,1)} %param.26) | copy-start | bytes 3145732
  7.2 68.1 %all-gather.9.cloned.1.call-start = ((), (), s32[]{:S(2)}) async-start(), calls=%async_computation.10 | async-start | bytes 1081344 | tf_op jit(solution)/shard_map/all_gather | solution.py:14
  15.5 39.7 %all-to-all-start.3 = ((bf16[16,16,128]{2,1,0:T(8,128)(2,1)}), bf16[16,16,128]{2,1,0:T(8,128)(2,1)S(1)}, u32[]{:S(2)}, u32[]{:S(2)}) async-start(bf16[16,16,128]{2,1,0:T(8,128)(2,1)} %bitcast.24), calls=%async_computation.4 | async-start | bytes 131072 | tf_op jit(solution)/shard_map/all_to_all | solution.py:126
  31.2 169.8 %all-gather.7.cloned.1.call-start = ((), (), s32[]{:S(2)}) async-start(), calls=%async_computation.8 | async-start | bytes 2162688 | tf_op jit(solution)/shard_map/all_gather | solution.py:132
  55.9 233.7 %reduce-scatter.3.cloned.1.call-start = ((), (), s32[]{:S(2)}) async-start(), calls=%async_computation.7 | async-start | bytes 2162688 | tf_op jit(solution)/shard_map/reduce_scatter | solution.py:139
  75.2 33.7 %copy-start.4 = (bf16[128,128]{1,0:T(8,128)(2,1)S(1)}, bf16[128,128]{1,0:T(8,128)(2,1)}, u32[]{:S(2)}) copy-start(bf16[128,128]{1,0:T(8,128)(2,1)} %param.19) | copy-start | bytes 98308
  75.2 34.1 %copy-start.10 = (f32[4]{0:T(128)S(1)}, f32[4]{0:T(128)}, u32[]{:S(2)}) copy-start(f32[4]{0:T(128)} %param.21) | copy-start | bytes 52
  75.2 34.7 %copy-start.6 = (bf16[128,128]{1,0:T(8,128)(2,1)S(1)}, bf16[128,128]{1,0:T(8,128)(2,1)}, u32[]{:S(2)}) copy-start(bf16[128,128]{1,0:T(8,128)(2,1)} %param.16) | copy-start | bytes 98308
  75.3 60.4 %copy-start.7 = (f32[128]{0:T(128)S(1)}, f32[128]{0:T(128)}, u32[]{:S(2)}) copy-start(f32[128]{0:T(128)} %param.22) | copy-start | bytes 1540
  155.3 42.7 %copy-start.2 = (bf16[1,2048,256]{2,1,0:T(8,128)(2,1)S(1)}, bf16[1,2048,256]{2,1,0:T(8,128)(2,1)}, u32[]{:S(2)}) copy-start(bf16[1,2048,256]{2,1,0:T(8,128)(2,1)} %param.25) | copy-start | bytes 3145732
  196.6 1.3 copy-start.1
  198.7 2.4 copy-start.11
  200.8 194.6 %reduce-scatter.5.cloned.1.call-start = ((), (), s32[]{:S(2)}) async-start(), calls=%async_computation.9 | async-start | bytes 2162688 | tf_op jit(solution)/shard_map/reduce_scatter | solution.py:161
  304.8 105.3 %all-to-all-start.2 = ((bf16[16,2,1024]{2,1,0:T(2,128)(2,1)}), bf16[16,2,1024]{2,1,0:T(2,128)(2,1)S(1)}, u32[]{:S(2)}, u32[]{:S(2)}) async-start(bf16[16,2,1024]{2,1,0:T(2,128)(2,1)} %reshape.211), calls=%async_computation.3 | async-start | bytes 131072 | tf_op jit(solution)/shard_map/all_to_all | solution.py:145
  410.1 23.6 %all-to-all-start.4 = ((bf16[16,2,1024]{2,1,0:T(2,128)(2,1)}), bf16[16,2,1024]{2,1,0:T(2,128)(2,1)S(1)}, u32[]{:S(2)}, u32[]{:S(2)}) async-start(bf16[16,2,1024]{2,1,0:T(2,128)(2,1)} %reshape.213), calls=%async_computation.6 | async-start | bytes 131072 | tf_op jit(solution)/shard_map/all_to_all | solution.py:169
  422.2 96.6 %all-gather.11.cloned.1.call-start = ((), (), s32[]{:S(2)}) async-start(), calls=%async_computation.11 | async-start | bytes 1081344 | tf_op jit(solution)/shard_map/all_gather | solution.py:14
  423.3 11.9 %copy-start.8 = (f32[128,2]{0,1:T(2,128)S(1)}, f32[128,2]{0,1:T(2,128)}, u32[]{:S(2)}) copy-start(f32[128,2]{0,1:T(2,128)} %param.23) | copy-start | bytes 3076
  423.9 33.6 %copy-start.5 = (bf16[128,128]{1,0:T(8,128)(2,1)S(1)}, bf16[128,128]{1,0:T(8,128)(2,1)}, u32[]{:S(2)}) copy-start(bf16[128,128]{1,0:T(8,128)(2,1)} %param.27) | copy-start | bytes 98308
  459.1 3.5 copy-start.9
  459.1 3.5 copy-start.12
  518.8 34.0 %copy-start.3 = (bf16[128,128]{1,0:T(8,128)(2,1)S(1)}, bf16[128,128]{1,0:T(8,128)(2,1)}, u32[]{:S(2)}) copy-start(bf16[128,128]{1,0:T(8,128)(2,1)} %param.18) | copy-start | bytes 98308
Sparse Core Ops, SparseCore 0:
  11.7 63.5 all-gather.8
  79.0 58.4 all-gather.6
  200.9 88.6 reduce-scatter.2
  293.9 101.4 reduce-scatter.4
  459.2 59.5 all-gather.10
